TPU v7x, 32 devices: a whole 2x2x4 slice. The times are simulated.
32 devices in a mesh: clip: 8 (over z, x), tm: 4 (over y, core).
Axes of the slice: x: 2, y: 2, z: 4, core: 2. Of those that a mesh axis runs over, the one named last changes fastest.
Arguments:
- features: bfloat16 [16, 1024, 512], P('clip', 'tm'), may hold values from -6 to 6
- cotangent: bfloat16 [16, 1024, 512], P('clip', 'tm'), may hold values from -6 to 6
- clip_lengths: int32 [16], P('clip'), may hold values from 128 to 1024, as said below
- code_ids: int32 [4, 16, 1024], P(None, 'clip', 'tm'), may hold values from 0 to 1023
- step_count: int32 [1], replicated, may hold values from 2 to 20
- dilated_kernel_weight: float32 [3, 512, 256], P(None, None, 'clip'), may hold values from -0.15625 to 0.15625
- pointwise_conv: float32 [256, 512], P(None, 'clip'), may hold values from -0.75 to 0.75
- codebooks: float32 [4, 1024, 256], P(None, 'clip'), may hold values from -6 to 6
- dilated_first_moment: float32 [3, 512, 256], P(None, None, 'clip'), may hold values from -1 to 1
- dilated_second_moment: float32 [3, 512, 256], P(None, None, 'clip'), may hold values from 0.028995216 to 0.11598086
- pointwise_first: float32 [256, 512], P(None, 'clip'), may hold values from -1 to 1
- pointwise_second: float32 [256, 512], P(None, 'clip'), may hold values from 0.028995216 to 0.11598086
- codebook_first: float32 [4, 1024, 256], P(None, 'clip'), may hold values from -0.01953125 to 0.01953125
- codebook_second: float32 [4, 1024, 256], P(None, 'clip'), may hold values from 9.745614e-06 to 3.8982456e-05
Outputs:
- quantized: bfloat16 [16, 1024, 512], P('clip', 'tm')
- features_gradient: float32 [16, 1024, 512], P('clip', 'tm')
- grad_norm: float32 [1], replicated
- dilated_new: float32 [3, 512, 256], P(None, None, 'clip')
- dilated_grad: float32 [3, 512, 256], P(None, None, 'clip')
- dilated_square: float32 [3, 512, 256], P(None, None, 'clip')
- pointwise_new: float32 [256, 512], P(None, 'clip')
- pointwise_grad: float32 [256, 512], P(None, 'clip')
- pointwise_square: float32 [256, 512], P(None, 'clip')
- codebook_new: float32 [4, 1024, 256], P(None, 'clip')
- codebook_grad: float32 [4, 1024, 256], P(None, 'clip')
- codebook_square: float32 [4, 1024, 256], P(None, 'clip')
Inputs may be any that keep to these rules, and one draw needn't show every extreme that they name: `clip_lengths`: the number of valid frames of each clip; frames from it on are padding; clip 0 is always full.
All inputs are finite; a program needn't handle non-finite values.
Results may differ from a plain program's by a relative error of at most 0.001.
The roundings to bfloat16 on the way count: a program that leaves them out, or rounds other values in their place, can miss the bound.
Values may be sent and summed in bfloat16 or wider, within the bound.
No kernel may reach another device: no remote copies, remote signals or barrier semaphores. Data moves between devices by JAX's collectives and lax.ppermute only.
A program may use at most 64 MiB of HBM per device.

v0:
```python
import jax
import jax.numpy as jnp
from jax import lax
from jax.sharding import PartitionSpec as P

HID = 256
CODES = 1024
GROUPS = 2
LEVELS = 2
KERNEL = 3
DILATION = 3
DG = 256
COMMIT = 0.25
FIRST_DECAY = 0.9
SECOND_DECAY = 0.99
EPSILON = 1e-08
WEIGHT_DECAY = 0.01
BITRATE_FACTOR = 0.02
RATE_CODE = 0.5


def extended(cells, sides, width):
    for axis, dim in sides:
        count = lax.axis_size(axis)
        ends = count - 1
        head = lax.slice_in_dim(cells, 0, width, axis=dim)
        tail = lax.slice_in_dim(cells, cells.shape[dim] - width, cells.shape[dim], axis=dim)
        cells = jnp.concatenate(
            [
                lax.ppermute(tail, axis, [(i, (i + 1) % count) for i in range(ends)]),
                cells,
                lax.ppermute(head, axis, [((i + 1) % count, i) for i in range(ends)]),
            ],
            axis=dim,
        )
    return cells


def elu_slope(values):
    return jnp.where(values > 0, 1.0, jnp.exp(jnp.minimum(values, 0.0)))


def adamw_update(weight, first, second, grad, rate, completed_steps):
    first_new = FIRST_DECAY * first + (1.0 - FIRST_DECAY) * grad
    second_new = SECOND_DECAY * second + (1.0 - SECOND_DECAY) * grad * grad
    first_hat = first_new / (1.0 - FIRST_DECAY**completed_steps)
    second_hat = second_new / (1.0 - SECOND_DECAY**completed_steps)
    weight_new = weight - rate * (
        first_hat / (jnp.sqrt(second_hat) + EPSILON) + WEIGHT_DECAY * weight
    )
    return (weight_new, grad, second_new)


def shards(
    features,
    cotangent,
    clip_lengths,
    code_ids,
    step_count,
    dilated_kernel_weight,
    pointwise_conv,
    codebooks,
    dilated_first_moment,
    dilated_second_moment,
    pointwise_first,
    pointwise_second,
    codebook_first,
    codebook_second,
):
    clip_rank = lax.axis_index("clip")
    time_rank = lax.axis_index("tm")
    dilated_full, pointwise_full, table_full = (
        lax.all_gather(dilated_kernel_weight.astype(jnp.bfloat16), "clip", axis=2, tiled=True),
        lax.all_gather(pointwise_conv.astype(jnp.bfloat16), "clip", axis=1, tiled=True),
        lax.all_gather(codebooks.astype(jnp.bfloat16), "clip", axis=1, tiled=True),
    )
    clips, frames, width = features.shape
    positions = time_rank * frames + lax.broadcasted_iota(jnp.int32, (clips, frames, 1), 1)
    frame_mask = (positions < clip_lengths[:, None, None]).astype(jnp.float32)
    start = features.astype(jnp.float32) * frame_mask
    activated = jax.nn.elu(start).astype(jnp.bfloat16)
    padded = extended(activated, (("tm", 1),), DILATION)
    hidden = jnp.zeros((clips, frames, HID), jnp.float32)
    for tap_index in range(KERNEL):
        window = padded[:, tap_index * DILATION : tap_index * DILATION + frames]
        hidden = hidden + jnp.einsum(
            "btc,cd->btd", window, dilated_full[tap_index], preferred_element_type=jnp.float32
        )
    gated = jax.nn.elu(hidden).astype(jnp.bfloat16)
    latent = start + jnp.einsum(
        "btk,kd->btd", gated, pointwise_full, preferred_element_type=jnp.float32
    )
    backs = cotangent.astype(jnp.float32) * frame_mask
    latent_parts = []
    quant_parts = []
    table_grads = []
    for group in range(GROUPS):
        residual_part = latent[..., group * DG : (group + 1) * DG]
        moving_grad = backs[..., group * DG : (group + 1) * DG]
        summed = jnp.zeros_like(residual_part)
        for level in range(LEVELS):
            slot = group * LEVELS + level
            chosen = jnp.take(table_full[slot], code_ids[slot], axis=0).astype(jnp.float32)
            moving_grad = moving_grad + 2.0 * COMMIT * frame_mask * (residual_part - chosen)
            code_grad = 2.0 * frame_mask * (chosen - residual_part)
            table_grads.append(
                jax.ops.segment_sum(
                    code_grad.reshape(-1, DG), code_ids[slot].reshape(-1), num_segments=CODES
                )
            )
            residual_part = residual_part - chosen
            summed = summed + chosen
        latent_parts.append(moving_grad)
        quant_parts.append(summed)
    quantized = (jnp.concatenate(quant_parts, axis=-1) * frame_mask).astype(jnp.bfloat16)
    latent_grad = jnp.concatenate(latent_parts, axis=-1)
    table_grad = jnp.stack(table_grads, axis=0)
    branch_grad = latent_grad.astype(jnp.bfloat16)
    pointwise_grad = jnp.einsum(
        "btk,btd->kd", gated, branch_grad, preferred_element_type=jnp.float32
    )
    gated_grad = jnp.einsum(
        "btd,kd->btk", branch_grad, pointwise_full, preferred_element_type=jnp.float32
    )
    hidden_grad = (gated_grad * elu_slope(hidden)).astype(jnp.bfloat16)
    padded_grad = extended(hidden_grad, (("tm", 1),), DILATION)
    dilated_parts = []
    act_grad = jnp.zeros((clips, frames, width), jnp.float32)
    for tap_index in range(KERNEL):
        window = padded[:, tap_index * DILATION : tap_index * DILATION + frames]
        dilated_parts.append(
            jnp.einsum("btc,btd->cd", window, hidden_grad, preferred_element_type=jnp.float32)
        )
        offset = (KERNEL - 1 - tap_index) * DILATION
        act_grad = act_grad + jnp.einsum(
            "btd,cd->btc",
            padded_grad[:, offset : offset + frames],
            dilated_full[tap_index],
            preferred_element_type=jnp.float32,
        )
    dilated_grad = jnp.stack(dilated_parts, axis=0)
    features_gradient = frame_mask * (latent_grad + elu_slope(start) * act_grad)
    local_grads = (dilated_grad, pointwise_grad, table_grad)
    whole = lax.psum((local_grads[0], local_grads[1], local_grads[2]), ("clip", "tm"))
    squared = sum((jnp.sum(piece * piece) for piece in whole))
    shares = (
        lax.dynamic_slice_in_dim(
            whole[0], clip_rank * dilated_kernel_weight.shape[2], dilated_kernel_weight.shape[2], 2
        ),
        lax.dynamic_slice_in_dim(
            whole[1], clip_rank * pointwise_conv.shape[1], pointwise_conv.shape[1], 1
        ),
        lax.dynamic_slice_in_dim(whole[2], clip_rank * codebooks.shape[1], codebooks.shape[1], 1),
    )
    count = dilated_full.size + pointwise_full.size + table_full.size
    limit = jnp.sqrt(jnp.float32(count))
    gradient_norm_total = jnp.sqrt(squared)
    clip_scale_factor = limit / jnp.maximum(gradient_norm_total, limit)
    completed_steps = step_count[0].astype(jnp.float32)
    dilation_factor = adamw_update(
        dilated_kernel_weight,
        dilated_first_moment,
        dilated_second_moment,
        shares[0] * clip_scale_factor,
        BITRATE_FACTOR,
        completed_steps,
    )
    pointwise_kernel = adamw_update(
        pointwise_conv,
        pointwise_first,
        pointwise_second,
        shares[1] * clip_scale_factor,
        BITRATE_FACTOR,
        completed_steps,
    )
    codebook_tensor = adamw_update(
        codebooks,
        codebook_first,
        codebook_second,
        shares[2] * clip_scale_factor,
        RATE_CODE,
        completed_steps,
    )
    return (
        quantized,
        features_gradient,
        gradient_norm_total.reshape(1),
        dilation_factor[0],
        dilation_factor[1],
        dilation_factor[2],
        pointwise_kernel[0],
        pointwise_kernel[1],
        pointwise_kernel[2],
        codebook_tensor[0],
        codebook_tensor[1],
        codebook_tensor[2],
    )


def solution(mesh):
    in_specs = (
        P("clip", "tm", None),
        P("clip", "tm", None),
        P("clip"),
        P(None, "clip", "tm"),
        P(),
        P(None, None, "clip"),
        P(None, "clip"),
        P(None, "clip", None),
        P(None, None, "clip"),
        P(None, None, "clip"),
        P(None, "clip"),
        P(None, "clip"),
        P(None, "clip", None),
        P(None, "clip", None),
    )
    out_specs = (
        P("clip", "tm", None),
        P("clip", "tm", None),
        P(),
        P(None, None, "clip"),
        P(None, None, "clip"),
        P(None, None, "clip"),
        P(None, "clip"),
        P(None, "clip"),
        P(None, "clip"),
        P(None, "clip", None),
        P(None, "clip", None),
        P(None, "clip", None),
    )
    return jax.shard_map(shards, mesh=mesh, in_specs=in_specs, out_specs=out_specs, check_vma=False)
```

profile of v0, /device:TPU:0, one launch (start us, length us, event | category | flops | bytes accessed | tf_op | source)
XLA Modules:
  0.0 310.3 jit_solution(5738353770341371367)
XLA Ops:
  7.2 1.8 convert_element_type.54
  9.8 2.8 convert_multiply_fusion.1
  14.0 3.0 collective-permute-start
  19.6 33.2 %all_gather.11 = bf16[256,512]{0,1:T(8,128)(2,1)S(1)} all-gather(bf16[256,64]{0,1:T(8,128)(2,1)S(1)} %convert_element_type.66), channel_id=1, replica_groups=mesh['clip'=8,'tm'=4] {'clip'}, dimensions={1}, use_global_device_ids=true | all-gather | bytes 294912 | tf_op jit(solution)/shard_map/all_gather | solution.py:74
  52.9 33.2 %all_gather.10 = bf16[3,512,256]{1,2,0:T(8,128)(2,1)S(1)} all-gather(bf16[3,512,32]{1,2,0:T(8,128)(2,1)S(1)} %convert_element_type.64), channel_id=1, replica_groups=mesh['clip'=8,'tm'=4] {'clip'}, dimensions={2}, use_global_device_ids=true | all-gather | bytes 884736 | tf_op jit(solution)/shard_map/all_gather | solution.py:73
  89.4 1.7 slice_bitcast_fusion.3
  91.1 2.6 gather_fusion.1
  93.7 2.6 gather_fusion
  96.2 2.6 gather_fusion.3
  98.8 1.9 gather_fusion.2
  100.8 3.3 %fusion.12 = (f32[2,256,256]{2,1,0:T(8,128)S(1)}, f32[2,256,256]{2,1,0:T(8,128)S(1)}, f32[2,256,256]{2,1,0:T(8,128)}, f32[2,256,256]{2,1,0:T(8,128)}, f32[2,256,...) fusion(f32[2,256,512]{2,1,0:T(8,128)S(1)} %copy-done, ...), kind=kLoop, calls=%fused_computation.50 | loop fusion | flops 3932160 | bytes 7346176 | tf_op jit(solution)/shard_map/add | solution.py:104
  106.1 4.2 %scatter_custom_fusion.3 = f32[1024,256]{1,0:T(8,128)S(1)} fusion(s32[512]{0:T(512)S(1)} %bitcast.135, f32[512,256]{1,0:T(8,128)} %bitcast.127, f32[]{:T(128)} %constant.35.clone.1), kind=kCustom, calls=%fused_computation.74 | custom fusion | flops 131072 | bytes 1049088 | tf_op jit(solution)/shard_map/scatter-add | solution.py:107
  110.4 4.8 %scatter_custom_fusion.2 = f32[1024,256]{1,0:T(8,128)} fusion(s32[512]{0:T(512)S(1)} %bitcast.134, f32[512,256]{1,0:T(8,128)} %bitcast.126, f32[]{:T(128)} %constant.35.clone.1), kind=kCustom, calls=%fused_computation.76 | custom fusion | flops 131072 | bytes 1049088 | tf_op jit(solution)/shard_map/scatter-add | solution.py:107
  115.1 4.8 %scatter_custom_fusion.1 = f32[1024,256]{1,0:T(8,128)} fusion(s32[512]{0:T(512)S(1)} %bitcast.133, f32[512,256]{1,0:T(8,128)} %bitcast.125, f32[]{:T(128)} %constant.35.clone.1), kind=kCustom, calls=%fused_computation.78 | custom fusion | flops 131072 | bytes 1049088 | tf_op jit(solution)/shard_map/scatter-add | solution.py:107
  119.9 4.8 %scatter_custom_fusion = f32[1024,256]{1,0:T(8,128)} fusion(s32[512]{0:T(512)S(1)} %bitcast.132, f32[512,256]{1,0:T(8,128)} %bitcast.124, f32[]{:T(128)} %constant.35.clone.1), kind=kCustom, calls=%fused_computation.80 | custom fusion | flops 131072 | bytes 1049088 | tf_op jit(solution)/shard_map/scatter-add | solution.py:107
  126.8 2.3 pad_maximum_fusion
  136.0 1.6 fusion.3
  137.6 149.0 %all-reduce.3.cloned.1.call-done = (f32[3,512,256]{1,2,0:T(8,128)}, f32[256,512]{0,1:T(8,128)}, f32[4,1024,256]{2,1,0:T(8,128)}) async-done(((f32[3,512,256]{1,2,0:T(8,128)}, f32[256,512]{0,1:T(8,128)}, f32[4,1024,256]{2,1,0:T(8,128)}), (f32[3,512,256]{1,2,0:T(8,128)}, f32[256,512]{0,1:T(8,128)}, f32[4,1024,256]{2,1,0:T(8,128)})) %all-reduce.3.cloned.1.call-update) | async-done | bytes 6291472 | tf_op jit(solution)/shard_map/psum | solution.py:144
  286.6 2.4 multiply_reduce_fusion.1
  289.0 1.8 multiply_reduce_fusion.2
  290.8 3.9 %multiply_reduce_fusion = f32[]{:T(128)} fusion(f32[4,1024,256]{2,1,0:T(8,128)} %get-tuple-element.39), kind=kLoop, calls=%fused_computation.9 | loop fusion | flops 2097151 | bytes 4194308 | tf_op jit(solution)/shard_map/reduce_sum | solution.py:145
  296.7 1.8 multiply_subtract_fusion.1
  298.5 1.5 multiply_subtract_fusion.2
  300.1 2.3 multiply_subtract_fusion
  (101 shorter events, 18.1 us)
Async XLA Ops:
  7.2 45.6 %copy-start.26 = (s32[2]{0:T(128)S(1)}, s32[2]{0:T(128)}, u32[]{:S(2)}) copy-start(s32[2]{0:T(128)} %param.18) | copy-start | bytes 28
  7.2 45.7 %copy-start.23 = (s32[4,2,256]{2,1,0:T(2,128)S(1)}, s32[4,2,256]{2,1,0:T(2,128)}, u32[]{:S(2)}) copy-start(s32[4,2,256]{2,1,0:T(2,128)} %param.19) | copy-start | bytes 24580
  7.2 82.2 %all-gather.2.cloned.1.call-start = ((), (), s32[]{:S(2)}) async-start(), calls=%async_computation | async-start | bytes 2359296 | tf_op jit(solution)/shard_map/all_gather | solution.py:75
  9.0 277.5 %all-reduce.3.cloned.1.call-start = ((), (), s32[]{:S(2)}) async-start(), calls=%async_computation.1 | async-start | bytes 12582912 | tf_op jit(solution)/shard_map/psum | solution.py:144
  9.8 78.2 %copy-start.11 = (bf16[2,256,512]{2,1,0:T(8,128)(2,1)S(1)}, bf16[2,256,512]{2,1,0:T(8,128)(2,1)}, u32[]{:S(2)}) copy-start(bf16[2,256,512]{2,1,0:T(8,128)(2,1)} %param.16) | copy-start | bytes 1572868
  12.7 73.8 %collective-permute-start.1 = (bf16[2,3,512]{2,1,0:T(4,128)(2,1)S(1)}, bf16[2,3,512]{2,1,0:T(4,128)(2,1)S(1)}, u32[]{:S(2)}, u32[]{:S(2)}) collective-permute-start(bf16[2,3,512]{2,1,0:T(4,128)(2,1)S(1)} %get-tuple-element.62), channel_id=1, source_target_pairs={{1,0},{2,1},{3,2},{5,4},{6,5},{7,6},{9,8},{10,9},{11,10},{13,12},{... | collective-permute-start | bytes 18440 | tf_op jit(solution)/shard_map/ppermute | solution.py:32
  14.0 72.9 %collective-permute-start = (bf16[2,3,512]{2,1,0:T(4,128)(2,1)S(1)}, bf16[2,3,512]{2,1,0:T(4,128)(2,1)S(1)}, u32[]{:S(2)}, u32[]{:S(2)}) collective-permute-start(bf16[2,3,512]{2,1,0:T(4,128)(2,1)S(1)} %get-tuple-element.61), channel_id=1, source_target_pairs={{0,1},{1,2},{2,3},{4,5},{5,6},{6,7},{8,9},{9,10},{10,11},{12,13},{... | collective-permute-start | bytes 18440 | tf_op jit(solution)/shard_map/ppermute | solution.py:30
  52.8 34.4 %copy-start.19 = (bf16[256,512]{0,1:T(8,128)(2,1)}, bf16[256,512]{0,1:T(8,128)(2,1)S(1)}, u32[]{:S(2)}) copy-start(bf16[256,512]{0,1:T(8,128)(2,1)S(1)} %all_gather.11) | copy-start | bytes 786436
  96.2 4.5 %copy-start = (f32[2,256,512]{2,1,0:T(8,128)S(1)}, f32[2,256,512]{2,1,0:T(8,128)}, u32[]{:S(2)}) copy-start(f32[2,256,512]{2,1,0:T(8,128)} %get-tuple-element.77) | copy-start | bytes 3145732
  129.1 4.2 %copy-start.6 = (f32[2,256,256]{2,1,0:T(8,128)S(1)}, f32[2,256,256]{2,1,0:T(8,128)}, u32[]{:S(2)}) copy-start(f32[2,256,256]{2,1,0:T(8,128)} %get-tuple-element.60) | copy-start | bytes 1572868
  129.1 6.9 %copy-start.8 = (f32[2,256,256]{2,1,0:T(8,128)S(1)}, f32[2,256,256]{2,1,0:T(8,128)}, u32[]{:S(2)}) copy-start(f32[2,256,256]{2,1,0:T(8,128)} %copy-done.7) | copy-start | bytes 1572868
  129.1 6.9 %copy-start.10 = (f32[2,256,256]{2,1,0:T(8,128)S(1)}, f32[2,256,256]{2,1,0:T(8,128)}, u32[]{:S(2)}) copy-start(f32[2,256,256]{2,1,0:T(8,128)} %copy-done.9) | copy-start | bytes 1572868
  130.0 6.0 %copy-start.12 = (bf16[2,256,512]{2,1,0:T(8,128)(2,1)S(1)}, bf16[2,256,512]{2,1,0:T(8,128)(2,1)}, u32[]{:S(2)}) copy-start(bf16[2,256,512]{2,1,0:T(8,128)(2,1)} %param.16) | copy-start | bytes 1572868
  130.0 4.2 %collective-permute-start.3 = (bf16[2,3,256]{2,1,0:T(4,128)(2,1)S(1)}, bf16[2,3,256]{2,1,0:T(4,128)(2,1)S(1)}, u32[]{:S(2)}, u32[]{:S(2)}) collective-permute-start(bf16[2,3,256]{2,1,0:T(4,128)(2,1)S(1)} %get-tuple-element.64), channel_id=1, source_target_pairs={{0,1},{1,2},{2,3},{4,5},{5,6},{6,7},{8,9},{9,10},{10,11},{12,13},{... | collective-permute-start | bytes 9224 | tf_op jit(solution)/shard_map/ppermute | solution.py:30
  131.4 4.5 %collective-permute-start.2 = (bf16[2,3,256]{2,1,0:T(4,128)(2,1)S(1)}, bf16[2,3,256]{2,1,0:T(4,128)(2,1)S(1)}, u32[]{:S(2)}, u32[]{:S(2)}) collective-permute-start(bf16[2,3,256]{2,1,0:T(4,128)(2,1)S(1)} %get-tuple-element.63), channel_id=1, source_target_pairs={{1,0},{2,1},{3,2},{5,4},{6,5},{7,6},{9,8},{10,9},{11,10},{13,12},{... | collective-permute-start | bytes 9224 | tf_op jit(solution)/shard_map/ppermute | solution.py:32
  137.5 159.1 %copy-start.13 = (f32[3,512,32]{1,2,0:T(8,128)S(1)}, f32[3,512,32]{1,2,0:T(8,128)}, u32[]{:S(2)}) copy-start(f32[3,512,32]{1,2,0:T(8,128)} %param.21) | copy-start | bytes 589828
  137.5 159.2 %copy-start.21 = (f32[3,512,32]{1,2,0:T(8,128)S(1)}, f32[3,512,32]{1,2,0:T(8,128)}, u32[]{:S(2)}) copy-start(f32[3,512,32]{1,2,0:T(8,128)} %param.24) | copy-start | bytes 589828
  137.5 159.2 %copy-start.22 = (f32[3,512,32]{1,2,0:T(8,128)S(1)}, f32[3,512,32]{1,2,0:T(8,128)}, u32[]{:S(2)}) copy-start(f32[3,512,32]{1,2,0:T(8,128)} %param.25) | copy-start | bytes 589828
  137.5 161.0 %copy-start.18 = (f32[256,64]{0,1:T(8,128)S(1)}, f32[256,64]{0,1:T(8,128)}, u32[]{:S(2)}) copy-start(f32[256,64]{0,1:T(8,128)} %param.22) | copy-start | bytes 196612
  137.5 161.0 %copy-start.24 = (f32[256,64]{0,1:T(8,128)S(1)}, f32[256,64]{0,1:T(8,128)}, u32[]{:S(2)}) copy-start(f32[256,64]{0,1:T(8,128)} %param.26) | copy-start | bytes 196612
  137.5 161.0 %copy-start.25 = (f32[256,64]{0,1:T(8,128)S(1)}, f32[256,64]{0,1:T(8,128)}, u32[]{:S(2)}) copy-start(f32[256,64]{0,1:T(8,128)} %param.27) | copy-start | bytes 196612
  137.6 162.5 %copy-start.4 = (f32[4,128,256]{2,1,0:T(8,128)S(1)}, f32[4,128,256]{2,1,0:T(8,128)}, u32[]{:S(2)}) copy-start(f32[4,128,256]{2,1,0:T(8,128)} %param.23) | copy-start | bytes 1572868
  137.6 162.5 %copy-start.14 = (f32[4,128,256]{2,1,0:T(8,128)S(1)}, f32[4,128,256]{2,1,0:T(8,128)}, u32[]{:S(2)}) copy-start(f32[4,128,256]{2,1,0:T(8,128)} %param.28) | copy-start | bytes 1572868
  137.6 162.5 %copy-start.15 = (f32[4,128,256]{2,1,0:T(8,128)S(1)}, f32[4,128,256]{2,1,0:T(8,128)}, u32[]{:S(2)}) copy-start(f32[4,128,256]{2,1,0:T(8,128)} %param.29) | copy-start | bytes 1572868
  (9 other events, 21.8 us)
Sparse Core Ops, SparseCore 0:
  10.8 58.7 all-gather.1
  129.2 157.3 all-reduce.2
where the time goes:
time: 311 us; the launch traced here: 310 us
  waiting for transfers between devices  150 us (48%)
  blocking collectives  66.4 us (21%)
  other arithmetic  48.1 us (15%)
  between operations  18.6 us (6%)
  local copies, waits for them, and re-layouts  12.2 us (4%)
  starting transfers between devices  7.34 us (2%)
  matrix products  7.32 us (2%)
    psum x1, waiting for transfers between devices, shards(): lax.psum((local_grads[0], local_grads[1], local_grads[2]), ('clip', 'tm'))  149 us
    all_gather x1, blocking collectives, shards(): lax.all_gather(pointwise_conv.astype(jnp.bfloat16), 'clip', axis=1, tiled...  33.2 us
    all_gather x1, blocking collectives, shards(): lax.all_gather(dilated_kernel_weight.astype(jnp.bfloat16), 'clip', axis=2...  33.2 us
    scatter-add x4, other arithmetic, shards(): jax.ops.segment_sum(code_grad.reshape(-1, DG), code_ids[slot].reshape(-1)...  18.6 us
    gather x4, local copies, waits for them, and re-layouts, shards(): jnp.take(table_full[slot], code_ids[slot], axis=0).astype(jnp.float32)  9.65 us
    reduce_sum x3, other arithmetic, shards(): squared = sum((jnp.sum(piece * piece) for piece in whole))  8.06 us
  transfers between devices with their start and end apart: 6, of which 2 were waited for; matrix products, arithmetic and copies ran while one was open for 4% of the time, Pallas kernels for 0%

commit v1 on v0

--- a/solution.py
+++ b/solution.py
@@ -141,7 +141,7 @@
     dilated_grad = jnp.stack(dilated_parts, axis=0)
     features_gradient = frame_mask * (latent_grad + elu_slope(start) * act_grad)
     local_grads = (dilated_grad, pointwise_grad, table_grad)
-    whole = lax.psum((local_grads[0], local_grads[1], local_grads[2]), ("clip", "tm"))
+    whole = lax.psum(lax.psum((local_grads[0], local_grads[1], local_grads[2]), "tm"), "clip")
     squared = sum((jnp.sum(piece * piece) for piece in whole))
     shares = (
         lax.dynamic_slice_in_dim(

time: 311 us -> 493 us (1.59)
  waiting for transfers between devices: 150 us -> 332 us
    psum x1 -> x2, waiting for transfers between devices: 149 us -> 331 us  [the longest x1 211 us: shards(): lax.psum(lax.psum((local_grads[0], local_grads[1], local_grads[2]), 'tm')...]
  transfers between devices with their start and end apart: 6 -> 7, of which waited for: 2 -> 3; matrix products, arithmetic and copies ran while one was open for 4% -> 2% of each run, Pallas kernels for 0% -> 0%
where the time goes in v1:
time: 493 us; the launch traced here: 492 us
  waiting for transfers between devices  332 us (67%)
  blocking collectives  66.4 us (13%)
  other arithmetic  48 us (10%)
  between operations  18.2 us (4%)
  local copies, waits for them, and re-layouts  12.3 us (2%)
  starting transfers between devices  7.61 us (2%)
  matrix products  7.33 us (1%)
    psum x1, waiting for transfers between devices, shards(): lax.psum(lax.psum((local_grads[0], local_grads[1], local_grads[2]), 'tm')...  211 us
    psum x1, waiting for transfers between devices, shards(): lax.psum((local_grads[0], local_grads[1], local_grads[2]), 'tm')  121 us
    all_gather x1, blocking collectives, shards(): lax.all_gather(pointwise_conv.astype(jnp.bfloat16), 'clip', axis=1, tiled...  33.2 us
    all_gather x1, blocking collectives, shards(): lax.all_gather(dilated_kernel_weight.astype(jnp.bfloat16), 'clip', axis=2...  33.2 us
    scatter-add x4, other arithmetic, shards(): jax.ops.segment_sum(code_grad.reshape(-1, DG), code_ids[slot].reshape(-1)...  18.6 us
  transfers between devices with their start and end apart: 7, of which 3 were waited for; matrix products, arithmetic and copies ran while one was open for 2% of the time, Pallas kernels for 0%

profile of v1, /device:TPU:0, one launch (start us, length us, event | category | flops | bytes accessed | tf_op | source)
XLA Modules:
  0.0 491.8 jit_solution(14045445107942005590)
XLA Ops:
  7.2 1.8 convert_element_type.54
  9.8 2.8 convert_multiply_fusion.1
  14.0 3.0 collective-permute-start
  19.6 33.2 %all_gather.11 = bf16[256,512]{0,1:T(8,128)(2,1)S(1)} all-gather(bf16[256,64]{0,1:T(8,128)(2,1)S(1)} %convert_element_type.66), channel_id=1, replica_groups=mesh['clip'=8,'tm'=4] {'clip'}, dimensions={1}, use_global_device_ids=true | all-gather | bytes 294912 | tf_op jit(solution)/shard_map/all_gather | solution.py:74
  52.9 33.2 %all_gather.10 = bf16[3,512,256]{1,2,0:T(8,128)(2,1)S(1)} all-gather(bf16[3,512,32]{1,2,0:T(8,128)(2,1)S(1)} %convert_element_type.64), channel_id=1, replica_groups=mesh['clip'=8,'tm'=4] {'clip'}, dimensions={2}, use_global_device_ids=true | all-gather | bytes 884736 | tf_op jit(solution)/shard_map/all_gather | solution.py:73
  89.5 1.7 slice_bitcast_fusion.3
  91.1 2.6 gather_fusion.1
  93.7 2.6 gather_fusion
  96.2 2.6 gather_fusion.3
  98.8 1.9 gather_fusion.2
  100.8 3.3 fusion.12
  106.1 4.2 scatter_custom_fusion.3
  110.4 4.8 scatter_custom_fusion.2
  115.1 4.8 scatter_custom_fusion.1
  120.0 4.8 scatter_custom_fusion
  126.8 2.3 pad_maximum_fusion
  129.1 120.9 %all-reduce.7.cloned.1.call-done = (f32[3,512,256]{1,2,0:T(8,128)}, f32[256,512]{0,1:T(8,128)}, f32[4,1024,256]{2,1,0:T(8,128)}) async-done(((f32[3,512,256]{1,2,0:T(8,128)}, f32[256,512]{0,1:T(8,128)}, f32[4,1024,256]{2,1,0:T(8,128)}), (f32[3,512,256]{1,2,0:T(8,128)}, f32[256,512]{0,1:T(8,128)}, f32[4,1024,256]{2,1,0:T(8,128)})) %all-reduce.7.cloned.1.call-update) | async-done | bytes 6291472 | tf_op jit(solution)/shard_map/psum | solution.py:144
  250.9 1.7 collective-permute-start.3
  257.8 210.5 %all-reduce.5.cloned.1.call-done = (f32[3,512,256]{1,2,0:T(8,128)}, f32[256,512]{0,1:T(8,128)}, f32[4,1024,256]{2,1,0:T(8,128)}) async-done(((f32[3,512,256]{1,2,0:T(8,128)}, f32[256,512]{0,1:T(8,128)}, f32[4,1024,256]{2,1,0:T(8,128)}), (f32[3,512,256]{1,2,0:T(8,128)}, f32[256,512]{0,1:T(8,128)}, f32[4,1024,256]{2,1,0:T(8,128)})) %all-reduce.5.cloned.1.call-update) | async-done | bytes 6291472 | tf_op jit(solution)/shard_map/psum | solution.py:144
  468.3 2.4 multiply_reduce_fusion.1
  470.7 1.8 multiply_reduce_fusion.2
  472.5 3.9 multiply_reduce_fusion
  478.4 1.8 multiply_subtract_fusion.1
  481.8 2.3 multiply_subtract_fusion
  (104 shorter events, 18.9 us)
Async XLA Ops:
  7.2 45.6 %copy-start.26 = (s32[2]{0:T(128)S(1)}, s32[2]{0:T(128)}, u32[]{:S(2)}) copy-start(s32[2]{0:T(128)} %param.18) | copy-start | bytes 28
  7.2 45.7 %copy-start.23 = (s32[4,2,256]{2,1,0:T(2,128)S(1)}, s32[4,2,256]{2,1,0:T(2,128)}, u32[]{:S(2)}) copy-start(s32[4,2,256]{2,1,0:T(2,128)} %param.19) | copy-start | bytes 24580
  7.2 82.3 %all-gather.2.cloned.1.call-start = ((), (), s32[]{:S(2)}) async-start(), calls=%async_computation | async-start | bytes 2359296 | tf_op jit(solution)/shard_map/all_gather | solution.py:75
  9.0 241.0 %all-reduce.7.cloned.1.call-start = ((), (), s32[]{:S(2)}) async-start(), calls=%async_computation.2 | async-start | bytes 12582912 | tf_op jit(solution)/shard_map/psum | solution.py:144
  9.8 78.2 %copy-start.11 = (bf16[2,256,512]{2,1,0:T(8,128)(2,1)S(1)}, bf16[2,256,512]{2,1,0:T(8,128)(2,1)}, u32[]{:S(2)}) copy-start(bf16[2,256,512]{2,1,0:T(8,128)(2,1)} %param.16) | copy-start | bytes 1572868
  12.7 73.8 %collective-permute-start.1 = (bf16[2,3,512]{2,1,0:T(4,128)(2,1)S(1)}, bf16[2,3,512]{2,1,0:T(4,128)(2,1)S(1)}, u32[]{:S(2)}, u32[]{:S(2)}) collective-permute-start(bf16[2,3,512]{2,1,0:T(4,128)(2,1)S(1)} %get-tuple-element.65), channel_id=1, source_target_pairs={{1,0},{2,1},{3,2},{5,4},{6,5},{7,6},{9,8},{10,9},{11,10},{13,12},{... | collective-permute-start | bytes 18440 | tf_op jit(solution)/shard_map/ppermute | solution.py:32
  14.0 72.9 %collective-permute-start = (bf16[2,3,512]{2,1,0:T(4,128)(2,1)S(1)}, bf16[2,3,512]{2,1,0:T(4,128)(2,1)S(1)}, u32[]{:S(2)}, u32[]{:S(2)}) collective-permute-start(bf16[2,3,512]{2,1,0:T(4,128)(2,1)S(1)} %get-tuple-element.64), channel_id=1, source_target_pairs={{0,1},{1,2},{2,3},{4,5},{5,6},{6,7},{8,9},{9,10},{10,11},{12,13},{... | collective-permute-start | bytes 18440 | tf_op jit(solution)/shard_map/ppermute | solution.py:30
  52.8 34.4 %copy-start.19 = (bf16[256,512]{0,1:T(8,128)(2,1)}, bf16[256,512]{0,1:T(8,128)(2,1)S(1)}, u32[]{:S(2)}) copy-start(bf16[256,512]{0,1:T(8,128)(2,1)S(1)} %all_gather.11) | copy-start | bytes 786436
  129.1 125.3 %copy-start.5 = (f32[2,256,256]{2,1,0:T(8,128)S(1)}, f32[2,256,256]{2,1,0:T(8,128)}, u32[]{:S(2)}) copy-start(f32[2,256,256]{2,1,0:T(8,128)} %get-tuple-element.62) | copy-start | bytes 1572868
  129.1 125.3 %copy-start.6 = (f32[2,256,256]{2,1,0:T(8,128)S(1)}, f32[2,256,256]{2,1,0:T(8,128)}, u32[]{:S(2)}) copy-start(f32[2,256,256]{2,1,0:T(8,128)} %get-tuple-element.63) | copy-start | bytes 1572868
  129.1 339.2 %all-reduce.5.cloned.1.call-start = ((), (), s32[]{:S(2)}) async-start(), calls=%async_computation.1 | async-start | bytes 12582912 | tf_op jit(solution)/shard_map/psum | solution.py:144
  250.0 6.1 %copy-start.8 = (f32[2,256,256]{2,1,0:T(8,128)S(1)}, f32[2,256,256]{2,1,0:T(8,128)}, u32[]{:S(2)}) copy-start(f32[2,256,256]{2,1,0:T(8,128)} %copy-done.7) | copy-start | bytes 1572868
  250.0 6.1 %copy-start.10 = (f32[2,256,256]{2,1,0:T(8,128)S(1)}, f32[2,256,256]{2,1,0:T(8,128)}, u32[]{:S(2)}) copy-start(f32[2,256,256]{2,1,0:T(8,128)} %copy-done.9) | copy-start | bytes 1572868
  250.9 4.4 collective-permute-start.3
  252.6 3.6 collective-permute-start.2
  257.7 220.7 %copy-start.13 = (f32[3,512,32]{1,2,0:T(8,128)S(1)}, f32[3,512,32]{1,2,0:T(8,128)}, u32[]{:S(2)}) copy-start(f32[3,512,32]{1,2,0:T(8,128)} %param.21) | copy-start | bytes 589828
  257.7 220.7 %copy-start.21 = (f32[3,512,32]{1,2,0:T(8,128)S(1)}, f32[3,512,32]{1,2,0:T(8,128)}, u32[]{:S(2)}) copy-start(f32[3,512,32]{1,2,0:T(8,128)} %param.24) | copy-start | bytes 589828
  257.7 220.7 %copy-start.22 = (f32[3,512,32]{1,2,0:T(8,128)S(1)}, f32[3,512,32]{1,2,0:T(8,128)}, u32[]{:S(2)}) copy-start(f32[3,512,32]{1,2,0:T(8,128)} %param.25) | copy-start | bytes 589828
  257.7 222.5 %copy-start.18 = (f32[256,64]{0,1:T(8,128)S(1)}, f32[256,64]{0,1:T(8,128)}, u32[]{:S(2)}) copy-start(f32[256,64]{0,1:T(8,128)} %param.22) | copy-start | bytes 196612
  257.7 222.5 %copy-start.24 = (f32[256,64]{0,1:T(8,128)S(1)}, f32[256,64]{0,1:T(8,128)}, u32[]{:S(2)}) copy-start(f32[256,64]{0,1:T(8,128)} %param.26) | copy-start | bytes 196612
  257.7 222.5 %copy-start.25 = (f32[256,64]{0,1:T(8,128)S(1)}, f32[256,64]{0,1:T(8,128)}, u32[]{:S(2)}) copy-start(f32[256,64]{0,1:T(8,128)} %param.27) | copy-start | bytes 196612
  257.8 224.0 %copy-start.4 = (f32[4,128,256]{2,1,0:T(8,128)S(1)}, f32[4,128,256]{2,1,0:T(8,128)}, u32[]{:S(2)}) copy-start(f32[4,128,256]{2,1,0:T(8,128)} %param.23) | copy-start | bytes 1572868
  257.8 224.0 %copy-start.14 = (f32[4,128,256]{2,1,0:T(8,128)S(1)}, f32[4,128,256]{2,1,0:T(8,128)}, u32[]{:S(2)}) copy-start(f32[4,128,256]{2,1,0:T(8,128)} %param.28) | copy-start | bytes 1572868
  257.8 224.0 %copy-start.15 = (f32[4,128,256]{2,1,0:T(8,128)S(1)}, f32[4,128,256]{2,1,0:T(8,128)}, u32[]{:S(2)}) copy-start(f32[4,128,256]{2,1,0:T(8,128)} %param.29) | copy-start | bytes 1572868
  (10 other events, 27.4 us)
Sparse Core Ops, SparseCore 0:
  10.8 58.7 all-gather.1
  129.2 120.7 all-reduce.6
  254.3 213.9 all-reduce.4
